TPU v7x, 256 devices: a whole 4x4x8 slice. The times are simulated.
256 devices in a mesh: wide: 32 (over y, x, core), narrow: 8 (over z).
Axes of the slice: x: 4, y: 4, z: 8, core: 2. Of those that a mesh axis runs over, the one named last changes fastest.
Arguments:
- three_centre: bfloat16 [32, 1024, 4096], P('narrow', 'wide'), may hold values from -6 to 6
- go_blocks: bfloat16 [64, 64, 64], replicated, may hold values from -0.75 to 0.75
- gv_blocks: bfloat16 [64, 64, 64], replicated, may hold values from -0.125 to 0.125
- go_index: int32 [32, 32], P('narrow'), may hold values from 0 to 63
- gv_index: int32 [32, 32], P('narrow'), may hold values from 0 to 63
- source_mask: int32 [32, 32], P('narrow'), may hold values 0 or 1
Outputs:
- chi: float32 [1024, 1024], P('wide', 'narrow')
All inputs are finite; a program needn't handle non-finite values. No bound on the sum of `source_mask` on one device may be relied on, other than what follows from the above.
Results may differ from a plain program's by a relative error of at most 0.004.
Values may be sent and summed in bfloat16 or wider, within the bound.
No kernel may reach another device: no remote copies, remote signals or barrier semaphores. Data moves between devices by JAX's collectives and lax.ppermute only.
A program may use at most 192 MiB of HBM per device.

v0:
```python
import jax
import jax.numpy as jnp
from jax import lax
from jax.sharding import PartitionSpec as P


def local(three_centre, go_blocks, gv_blocks, go_index, gv_index, source_mask):
    local_pairs, aux_local, pair_width = three_centre.shape
    block = go_blocks.shape[1]
    go_chosen = go_blocks[go_index]
    gv_chosen = gv_blocks[gv_index] * source_mask.astype(jnp.bfloat16)[:, :, None, None]
    piece = lax.all_gather(three_centre, "narrow", axis=0, tiled=True)
    number_sources = piece.shape[0]
    sources = piece.reshape(number_sources, aux_local, block, block)
    results = []
    for target in range(local_pairs):
        first_product = jnp.einsum(
            "cma,cpmn->cpan", go_chosen[target], sources, preferred_element_type=jnp.float32
        ).astype(jnp.bfloat16)
        results.append(
            jnp.einsum(
                "cpan,cnd->pad",
                first_product,
                gv_chosen[target],
                preferred_element_type=jnp.float32,
            )
        )
    summed = jnp.stack(results)
    image = summed.reshape(local_pairs, aux_local, pair_width).astype(jnp.bfloat16)
    norm_scale = 1.0 / jnp.sqrt(jnp.float32(local_pairs * lax.axis_size("narrow") * pair_width))
    partial_chi = jnp.einsum(
        "kpe,kqe->pq",
        image,
        lax.all_gather(three_centre, "wide", axis=1, tiled=True),
        preferred_element_type=jnp.float32,
    )
    result = lax.psum_scatter(partial_chi, "narrow", scatter_dimension=1, tiled=True)
    return result * norm_scale


def solution(mesh):
    placed = (
        P("narrow", "wide", None),
        P(),
        P(),
        P("narrow", None),
        P("narrow", None),
        P("narrow", None),
    )
    return jax.shard_map(
        local, mesh=mesh, in_specs=placed, out_specs=P("wide", "narrow"), check_vma=False
    )
```

profile of v0, /device:TPU:12, one launch (start us, length us, event | category | flops | bytes accessed | tf_op | source)
XLA Modules:
  0.0 286.2 jit_solution(9310431331818708807)
XLA Ops:
  6.5 0.7 all-gather.3.cloned.1.call-update
  7.3 0.7 all-gather.5.cloned.1.call-update
  8.1 0.7 compare_select_fusion
  8.7 0.1 reshape.28
  8.8 0.7 convert_element_type.30
  9.5 0.7 compare_select_fusion.1
  10.2 0.1 reshape.20
  10.3 1.0 gather_fusion.1
  11.3 3.4 %gather_fusion = bf16[128,64,64]{2,1,0:T(8,128)(2,1)} fusion(bf16[64,64,64]{2,1,0:T(8,128)(2,1)} %param.7, s32[1024]{0:T(1024)S(1)} %pad_clamp_fusion.1), kind=kCustom, calls=%fused_computation | custom fusion | bytes 2097664 | tf_op jit(solution)/shard_map/gather | solution.py:10
  14.7 1.5 broadcast_multiply_fusion
  16.2 90.0 %all-gather.3.cloned.1.call-done = bf16[32,32,4096]{2,1,0:T(8,128)(2,1)} async-done(((bf16[4,32,4096]{2,1,0:T(8,128)(2,1)}), bf16[32,32,4096]{2,1,0:T(8,128)(2,1)}) %all-gather.3.cloned.1.call-update) | async-done | bytes 8388624 | tf_op jit(solution)/shard_map/all_gather | solution.py:12
  106.2 23.6 %reshape.17 = bf16[32,32,64,64]{3,2,1,0:T(8,128)(2,1)} reshape(bf16[32,32,4096]{2,1,0:T(8,128)(2,1)} %all-gather.3.cloned.1.call-done) | data formatting | bytes 16777216 | tf_op jit(solution)/shard_map/reshape | solution.py:14
  129.8 10.7 %fusion.63 = bf16[32,64,64]{2,1,0:T(8,128)(2,1)S(1)} fusion(bf16[32,32,64,64]{3,2,1,0:T(8,128)(2,1)} %reshape.17, bf16[4,32,64,64]{3,2,1,0:T(8,128)(2,1)S(1)} %copy-done.2, bf16[128,64,64]{2,1,0:T(8,128)(2,1)} %gather_fusion), kind=kOutput, calls=%fused_computation.29 | convolution fusion | flops 1078067200 | bytes 18087936 | tf_op jit(solution)/shard_map/cpan,cnd->pad/dot_general | solution.py:21
  140.6 0.5 stack.15
  141.0 10.6 %fusion.58 = bf16[32,64,64]{2,1,0:T(8,128)(2,1)S(1)} fusion(bf16[32,32,64,64]{3,2,1,0:T(8,128)(2,1)} %reshape.17, bf16[4,32,64,64]{3,2,1,0:T(8,128)(2,1)S(1)} %copy-done.2, bf16[128,64,64]{2,1,0:T(8,128)(2,1)} %gather_fusion), kind=kOutput, calls=%fused_computation.28 | convolution fusion | flops 1078067200 | bytes 18087936 | tf_op jit(solution)/shard_map/cpan,cnd->pad/dot_general | solution.py:21
  151.6 1.2 stack.16
  152.8 12.7 %fusion.53 = bf16[32,64,64]{2,1,0:T(8,128)(2,1)S(1)} fusion(bf16[32,32,64,64]{3,2,1,0:T(8,128)(2,1)} %reshape.17, bf16[4,32,64,64]{3,2,1,0:T(8,128)(2,1)S(1)} %copy-done.2, bf16[128,64,64]{2,1,0:T(8,128)(2,1)} %gather_fusion), kind=kOutput, calls=%fused_computation.27 | convolution fusion | flops 1078067200 | bytes 18087936 | tf_op jit(solution)/shard_map/cpan,cnd->pad/dot_general | solution.py:21
  165.5 1.2 stack.17
  166.7 11.7 %fusion.48 = bf16[32,64,64]{2,1,0:T(8,128)(2,1)} fusion(bf16[32,32,64,64]{3,2,1,0:T(8,128)(2,1)} %reshape.17, bf16[4,32,64,64]{3,2,1,0:T(8,128)(2,1)S(1)} %copy-done.2, bf16[128,64,64]{2,1,0:T(8,128)(2,1)} %gather_fusion), kind=kOutput, calls=%fused_computation.26 | convolution fusion | flops 1078067200 | bytes 18087936 | tf_op jit(solution)/shard_map/cpan,cnd->pad/dot_general | solution.py:21
  178.4 1.6 stack.18
  180.0 44.6 %all-gather.5.cloned.1.call-done = bf16[4,1024,4096]{2,1,0:T(8,128)(2,1)} async-done(((bf16[4,32,4096]{2,1,0:T(8,128)(2,1)}), bf16[4,1024,4096]{2,1,0:T(8,128)(2,1)}) %all-gather.5.cloned.1.call-update) | async-done | bytes 33554448 | tf_op jit(solution)/shard_map/all_gather | solution.py:34
  224.6 16.0 %convolution_bitcast_fusion = f32[32,1024]{1,0:T(8,128)} fusion(bf16[4,1024,4096]{2,1,0:T(8,128)(2,1)} %all-gather.5.cloned.1.call-done, bf16[1,32,4096]{2,1,0:T(8,128)(2,1)S(1)} %stack.18, bf16[1,32,4096]{2,1,0:T(8,128)(2,1)} %stack.17, bf16[1,32,4096]{2,1,0:T(8,128)(2,1)} %stack.16, bf16[1,32,4096]{2,1,0:T(8,128)(2,1)S(1)} %stack.15), kind=kOutput, calls=%fused_computation.30 | convolution fusion | flops 1075314688 | bytes 34734080 | tf_op jit(solution)/shard_map/kpe,kqe->pq/dot_general | solution.py:31
  240.6 37.7 %reduce-scatter.2.cloned.1.call-done = f32[32,128]{1,0:T(8,128)} async-done(((f32[32,1024]{1,0:T(8,128)}), f32[32,128]{1,0:T(8,128)}) %reduce-scatter.2.cloned.1.call-update) | async-done | bytes 16400 | tf_op jit(solution)/shard_map/reduce_scatter | solution.py:37
  278.4 1.3 broadcast_multiply_fusion.1
  (12 shorter events, 0.1 us)
Async XLA Ops:
  6.5 3.8 %copy-start = (bf16[64,64,64]{2,1,0:T(8,128)(2,1)S(1)}, bf16[64,64,64]{2,1,0:T(8,128)(2,1)}, u32[]{:S(2)}) copy-start(bf16[64,64,64]{2,1,0:T(8,128)(2,1)} %param.8) | copy-start | bytes 1572868
  6.5 99.6 %all-gather.3.cloned.1.call-start = ((), (), s32[]{:S(2)}) async-start(), calls=%async_computation.1 | async-start | bytes 9437184 | tf_op jit(solution)/shard_map/all_gather | solution.py:12
  7.3 217.3 %all-gather.5.cloned.1.call-start = ((), (), s32[]{:S(2)}) async-start(), calls=%async_computation.2 | async-start | bytes 34603008 | tf_op jit(solution)/shard_map/all_gather | solution.py:34
  8.0 270.4 %reduce-scatter.2.cloned.1.call-start = ((), (), s32[]{:S(2)}) async-start(), calls=%async_computation.3 | async-start | bytes 147456 | tf_op jit(solution)/shard_map/reduce_scatter | solution.py:37
  16.2 113.6 %copy-start.2 = (bf16[4,32,64,64]{3,2,1,0:T(8,128)(2,1)S(1)}, bf16[4,32,64,64]{3,2,1,0:T(8,128)(2,1)}, u32[]{:S(2)}) copy-start(bf16[4,32,64,64]{3,2,1,0:T(8,128)(2,1)} %broadcast_multiply_fusion) | copy-start | bytes 3145732
  178.4 101.3 %copy-start.1 = (bf16[64,64,64]{2,1,0:T(8,128)(2,1)S(1)}, bf16[64,64,64]{2,1,0:T(8,128)(2,1)}, u32[]{:S(2)}) copy-start(bf16[64,64,64]{2,1,0:T(8,128)(2,1)} %param.8) | copy-start | bytes 1572868
Sparse Core Ops, SparseCore 0:
  9.1 96.9 all-gather.2
  108.8 115.7 all-gather.4
  240.7 37.5 reduce-scatter.1
where the time goes:
time: 287 us; the launch traced here: 286 us
  waiting for transfers between devices  174 us (61%)
  matrix products  61.8 us (22%)
  local copies, waits for them, and re-layouts  32.6 us (11%)
  between operations  13.2 us (5%)
  other arithmetic  4.92 us (2%)
    all_gather x1, waiting for transfers between devices, local(): piece = lax.all_gather(three_centre, 'narrow', axis=0, tiled=True)  90 us
    dot_general x4, matrix products, local(): jnp.einsum('cpan,cnd->pad', first_product, gv_chosen[target], preferred_e...  45.7 us
    all_gather x1, waiting for transfers between devices, local(): lax.all_gather(three_centre, 'wide', axis=1, tiled=True)  44.6 us
    reduce_scatter x1, waiting for transfers between devices, local(): lax.psum_scatter(partial_chi, 'narrow', scatter_dimension=1, tiled=True)  37.7 us
    reshape x1, local copies, waits for them, and re-layouts, local(): sources = piece.reshape(number_sources, aux_local, block, block)  23.6 us
    dot_general x1, matrix products, local(): jnp.einsum('kpe,kqe->pq', image, lax.all_gather(three_centre, 'wide', axi...  16 us
  transfers between devices with their start and end apart: 3, of which 3 were waited for; matrix products, arithmetic and copies ran while one was open for 29% of the time, Pallas kernels for 0%

commit v1 on v0

--- a/solution.py
+++ b/solution.py
@@ -2,6 +2,12 @@
 import jax.numpy as jnp
 from jax import lax
 from jax.sharding import PartitionSpec as P
+
+
+def joined_along(blocks, dim):
+    shape = list(blocks.shape[1:])
+    shape[dim] *= blocks.shape[0]
+    return jnp.moveaxis(blocks, 0, dim).reshape(shape)
 
 
 def local(three_centre, go_blocks, gv_blocks, go_index, gv_index, source_mask):
@@ -9,7 +15,19 @@
     block = go_blocks.shape[1]
     go_chosen = go_blocks[go_index]
     gv_chosen = gv_blocks[gv_index] * source_mask.astype(jnp.bfloat16)[:, :, None, None]
-    piece = lax.all_gather(three_centre, "narrow", axis=0, tiled=True)
+    count = lax.axis_size("narrow")
+    pairs = [(i, (i + 1) % count) for i in range(count)]
+    back = [(b, a) for a, b in pairs]
+    lower, upper = ([], [])
+    for hop in range(count - 1):
+        if hop % 2 == 0:
+            lower.append(lax.ppermute(lower[-1] if lower else three_centre, "narrow", pairs))
+        else:
+            upper.append(lax.ppermute(upper[-1] if upper else three_centre, "narrow", back))
+    tiles = jnp.stack([*lower[::-1], three_centre, *upper])
+    shift = lax.axis_index("narrow") - len(lower)
+    tiles = tiles[(jnp.arange(count) - shift) % count]
+    piece = joined_along(tiles, 0)
     number_sources = piece.shape[0]
     sources = piece.reshape(number_sources, aux_local, block, block)
     results = []

time: 287 us -> 266 us (0.927)
  waiting for transfers between devices: 174 us -> 120 us
  local copies, waits for them, and re-layouts: 32.6 us -> 55.5 us
  starting transfers between devices: 0.08 us -> 11.7 us
  matrix products: 61.8 us -> 58.4 us
    all_gather x1 -> x0, waiting for transfers between devices: 90 us -> none  [local(): piece = lax.all_gather(three_centre, 'narrow', axis=0, tiled=True)]
    ppermute x0 -> x7, waiting for transfers between devices: none -> 83.6 us  [the longest x4 83.6 us: local(): lax.ppermute(lower[-1] if lower else three_centre, 'narrow', pairs)]
    all_gather x1, waiting for transfers between devices: 44.6 us -> 0.02 us  [local(): lax.all_gather(three_centre, 'wide', axis=1, tiled=True)]
    another operation x0 -> x2, local copies, waits for them, and re-layouts: none -> 24.9 us  [the longest x1 23.8 us: local(): sources = piece.reshape(number_sources, aux_local, block, block)]
    reshape x1 -> x0, local copies, waits for them, and re-layouts: 23.6 us -> none  [local(): sources = piece.reshape(number_sources, aux_local, block, block)]
    unnamed x6 -> x23, local copies, waits for them, and re-layouts: 0.01 us -> 14.4 us
    ppermute x0 -> x7, starting transfers between devices: none -> 11.7 us  [the longest x3 9.69 us: local(): lax.ppermute(upper[-1] if upper else three_centre, 'narrow', back)]
    gather x0 -> x1, local copies, waits for them, and re-layouts: none -> 8.41 us  [local(): tiles = tiles[(jnp.arange(count) - shift) % count]]
  transfers between devices with their start and end apart: 3 -> 9, of which waited for: 3 -> 5; matrix products, arithmetic and copies ran while one was open for 29% -> 38% of each run, Pallas kernels for 0% -> 0%
where the time goes in v1:
time: 266 us; the launch traced here: 264 us
  waiting for transfers between devices  120 us (45%)
  matrix products  58.4 us (22%)
  local copies, waits for them, and re-layouts  55.5 us (21%)
  between operations  13.5 us (5%)
  starting transfers between devices  11.7 us (4%)
  other arithmetic  4.95 us (2%)
    ppermute x4, waiting for transfers between devices, local(): lax.ppermute(lower[-1] if lower else three_centre, 'narrow', pairs)  83.6 us
    dot_general x4, matrix products, local(): jnp.einsum('cpan,cnd->pad', first_product, gv_chosen[target], preferred_e...  42.3 us
    reduce_scatter x1, waiting for transfers between devices, local(): lax.psum_scatter(partial_chi, 'narrow', scatter_dimension=1, tiled=True)  35.9 us
    another operation x1, local copies, waits for them, and re-layouts, local(): sources = piece.reshape(number_sources, aux_local, block, block)  23.8 us
    dot_general x1, matrix products, local(): jnp.einsum('kpe,kqe->pq', image, lax.all_gather(three_centre, 'wide', axi...  16.1 us
    unnamed x23, local copies, waits for them, and re-layouts  14.4 us
    ppermute x3, starting transfers between devices, local(): lax.ppermute(upper[-1] if upper else three_centre, 'narrow', back)  9.69 us
    gather x1, local copies, waits for them, and re-layouts, local(): tiles = tiles[(jnp.arange(count) - shift) % count]  8.41 us
  transfers between devices with their start and end apart: 9, of which 5 were waited for; matrix products, arithmetic and copies ran while one was open for 38% of the time, Pallas kernels for 0%

profile of v1, /device:TPU:12, one launch (start us, length us, event | category | flops | bytes accessed | tf_op | source)
XLA Modules:
  0.0 264.4 jit_solution(8585225187400435794)
XLA Ops:
  7.3 2.0 collective-permute-start
  9.3 27.3 %collective-permute-done = bf16[4,32,4096]{2,1,0:T(8,128)(2,1)S(1)} collective-permute-done((bf16[4,32,4096]{2,1,0:T(8,128)(2,1)}, bf16[4,32,4096]{2,1,0:T(8,128)(2,1)S(1)}, u32[]{:S(2)}, u32[]{:S(2)}) %collective-permute-start) | collective-permute-done | bytes 1048608 | tf_op jit(solution)/shard_map/ppermute | solution.py:24
  37.6 3.2 %collective-permute-start.4 = (bf16[4,32,4096]{2,1,0:T(8,128)(2,1)}, bf16[4,32,4096]{2,1,0:T(8,128)(2,1)}, u32[]{:S(2)}, u32[]{:S(2)}) collective-permute-start(bf16[4,32,4096]{2,1,0:T(8,128)(2,1)} %param.6), channel_id=1, source_target_pairs={{1,0},{2,1},{3,2},{4,3},{5,4},{6,5},{7,6},{0,7},{9,8},{10,9},{11,1... | collective-permute-start | bytes 3145736 | tf_op jit(solution)/shard_map/ppermute | solution.py:26
  40.8 22.3 %collective-permute-done.1 = bf16[4,32,4096]{2,1,0:T(8,128)(2,1)S(1)} collective-permute-done((bf16[4,32,4096]{2,1,0:T(8,128)(2,1)S(1)}, bf16[4,32,4096]{2,1,0:T(8,128)(2,1)S(1)}, u32[]{:S(2)}, u32[]{:S(2)}) %collective-permute-start.1) | collective-permute-done | bytes 1048608 | tf_op jit(solution)/shard_map/ppermute | solution.py:24
  64.1 3.2 %collective-permute-start.5 = (bf16[4,32,4096]{2,1,0:T(8,128)(2,1)}, bf16[4,32,4096]{2,1,0:T(8,128)(2,1)}, u32[]{:S(2)}, u32[]{:S(2)}) collective-permute-start(bf16[4,32,4096]{2,1,0:T(8,128)(2,1)} %collective-permute-done.4), channel_id=1, source_target_pairs={{1,0},{2,1},{3,2},{4,3},{5,4},{6,5},{7,6},{0,7},{9,8},{10,9},{11,1... | collective-permute-start | bytes 3145736 | tf_op jit(solution)/shard_map/ppermute | solution.py:26
  67.3 21.5 %collective-permute-done.2 = bf16[4,32,4096]{2,1,0:T(8,128)(2,1)} collective-permute-done((bf16[4,32,4096]{2,1,0:T(8,128)(2,1)S(1)}, bf16[4,32,4096]{2,1,0:T(8,128)(2,1)}, u32[]{:S(2)}, u32[]{:S(2)}) %collective-permute-start.2) | collective-permute-done | bytes 1048608 | tf_op jit(solution)/shard_map/ppermute | solution.py:24
  92.1 3.5 %gather_fusion.1 = bf16[128,64,64]{2,1,0:T(8,128)(2,1)} fusion(bf16[64,64,64]{2,1,0:T(8,128)(2,1)} %param.7, s32[1024]{0:T(1024)S(1)} %pad_clamp_fusion.1), kind=kCustom, calls=%fused_computation.1 | custom fusion | bytes 2097664 | tf_op jit(solution)/shard_map/gather | solution.py:16
  95.6 1.5 broadcast_multiply_fusion
  97.1 3.2 %collective-permute-start.6 = (bf16[4,32,4096]{2,1,0:T(8,128)(2,1)}, bf16[4,32,4096]{2,1,0:T(8,128)(2,1)S(1)}, u32[]{:S(2)}, u32[]{:S(2)}) collective-permute-start(bf16[4,32,4096]{2,1,0:T(8,128)(2,1)} %collective-permute-done.5), channel_id=1, source_target_pairs={{1,0},{2,1},{3,2},{4,3},{5,4},{6,5},{7,6},{0,7},{9,8},{10,9},{11,1... | collective-permute-start | bytes 3145736 | tf_op jit(solution)/shard_map/ppermute | solution.py:26
  100.3 12.5 %collective-permute-done.3 = bf16[4,32,4096]{2,1,0:T(8,128)(2,1)} collective-permute-done((bf16[4,32,4096]{2,1,0:T(8,128)(2,1)}, bf16[4,32,4096]{2,1,0:T(8,128)(2,1)}, u32[]{:S(2)}, u32[]{:S(2)}) %collective-permute-start.3) | collective-permute-done | bytes 1048608 | tf_op jit(solution)/shard_map/ppermute | solution.py:24
  112.8 2.3 bitcast_dynamic-update-slice_fusion.7
  115.2 2.3 bitcast_dynamic-update-slice_fusion.6
  120.7 2.3 bitcast_dynamic-update-slice_fusion.2
  123.0 2.3 bitcast_dynamic-update-slice_fusion.1
  126.4 8.4 %gather_fusion = bf16[8,4,32,4096]{3,2,1,0:T(8,128)(2,1)} fusion(bf16[8,4,32,4096]{3,2,1,0:T(8,128)(2,1)} %bitcast_dynamic-update-slice_fusion, s32[1024]{0:T(1024)S(1)} %pad_clamp_fusion.2), kind=kCustom, calls=%fused_computation | custom fusion | bytes 16777248 | tf_op jit(solution)/shard_map/gather | solution.py:29
  134.8 23.8 %reshape_reshape.3 = bf16[32,32,64,64]{3,2,1,0:T(8,128)(2,1)} reshape(bf16[8,4,32,4096]{3,2,1,0:T(8,128)(2,1)} %gather_fusion) | data formatting | bytes 16777216 | tf_op jit(solution)/shard_map/reshape;reshape | solution.py:32
  158.6 10.6 %fusion.63 = bf16[32,64,64]{2,1,0:T(8,128)(2,1)S(1)} fusion(bf16[32,32,64,64]{3,2,1,0:T(8,128)(2,1)} %reshape_reshape.3, bf16[4,32,64,64]{3,2,1,0:T(8,128)(2,1)S(1)} %copy-done.3, bf16[128,64,64]{2,1,0:T(8,128)(2,1)} %gather_fusion.1), kind=kOutput, calls=%fused_computation.30 | convolution fusion | flops 1078067200 | bytes 18087936 | tf_op jit(solution)/shard_map/cpan,cnd->pad/dot_general | solution.py:39
  169.6 10.6 %fusion.58 = bf16[32,64,64]{2,1,0:T(8,128)(2,1)S(1)} fusion(bf16[32,32,64,64]{3,2,1,0:T(8,128)(2,1)} %reshape_reshape.3, bf16[4,32,64,64]{3,2,1,0:T(8,128)(2,1)S(1)} %copy-done.3, bf16[128,64,64]{2,1,0:T(8,128)(2,1)} %gather_fusion.1), kind=kOutput, calls=%fused_computation.29 | convolution fusion | flops 1078067200 | bytes 18087936 | tf_op jit(solution)/shard_map/cpan,cnd->pad/dot_general | solution.py:39
  180.2 1.2 stack.52
  181.4 10.6 %fusion.53 = bf16[32,64,64]{2,1,0:T(8,128)(2,1)S(1)} fusion(bf16[32,32,64,64]{3,2,1,0:T(8,128)(2,1)} %reshape_reshape.3, bf16[4,32,64,64]{3,2,1,0:T(8,128)(2,1)S(1)} %copy-done.3, bf16[128,64,64]{2,1,0:T(8,128)(2,1)} %gather_fusion.1), kind=kOutput, calls=%fused_computation.28 | convolution fusion | flops 1078067200 | bytes 18087936 | tf_op jit(solution)/shard_map/cpan,cnd->pad/dot_general | solution.py:39
  193.1 10.6 %fusion.48 = bf16[32,64,64]{2,1,0:T(8,128)(2,1)S(1)} fusion(bf16[32,32,64,64]{3,2,1,0:T(8,128)(2,1)} %reshape_reshape.3, bf16[4,32,64,64]{3,2,1,0:T(8,128)(2,1)S(1)} %copy-done.3, bf16[128,64,64]{2,1,0:T(8,128)(2,1)} %gather_fusion.1), kind=kOutput, calls=%fused_computation.27 | convolution fusion | flops 1078067200 | bytes 18087936 | tf_op jit(solution)/shard_map/cpan,cnd->pad/dot_general | solution.py:39
  204.2 16.1 %convolution_bitcast_fusion = f32[32,1024]{1,0:T(8,128)} fusion(bf16[4,1024,4096]{2,1,0:T(8,128)(2,1)} %all-gather.2.cloned.1.call-done, bf16[1,32,4096]{2,1,0:T(8,128)(2,1)S(1)} %stack.54, bf16[1,32,4096]{2,1,0:T(8,128)(2,1)} %stack.53, bf16[1,32,4096]{2,1,0:T(8,128)(2,1)} %stack.52, bf16[1,32,4096]{2,1,0:T(8,128)(2,1)S(1)} %stack.51), kind=kOutput, calls=%fused_computation.31 | convolution fusion | flops 1075314688 | bytes 34734080 | tf_op jit(solution)/shard_map/kpe,kqe->pq/dot_general | solution.py:49
  220.3 35.9 %reduce-scatter.2.cloned.1.call-done = f32[32,128]{1,0:T(8,128)} async-done(((f32[32,1024]{1,0:T(8,128)}), f32[32,128]{1,0:T(8,128)}) %reduce-scatter.2.cloned.1.call-update) | async-done | bytes 16400 | tf_op jit(solution)/shard_map/reduce_scatter | solution.py:55
  256.3 1.3 broadcast_multiply_fusion.1
  (44 shorter events, 12.4 us)
Async XLA Ops:
  6.5 84.5 %copy-start = (bf16[64,64,64]{2,1,0:T(8,128)(2,1)S(1)}, bf16[64,64,64]{2,1,0:T(8,128)(2,1)}, u32[]{:S(2)}) copy-start(bf16[64,64,64]{2,1,0:T(8,128)(2,1)} %param.8) | copy-start | bytes 1572868
  6.5 197.7 %all-gather.2.cloned.1.call-start = ((), (), s32[]{:S(2)}) async-start(), calls=%async_computation.1 | async-start | bytes 34603008 | tf_op jit(solution)/shard_map/all_gather | solution.py:52
  7.3 249.0 %reduce-scatter.2.cloned.1.call-start = ((), (), s32[]{:S(2)}) async-start(), calls=%async_computation.2 | async-start | bytes 147456 | tf_op jit(solution)/shard_map/reduce_scatter | solution.py:55
  7.3 29.3 %collective-permute-start = (bf16[4,32,4096]{2,1,0:T(8,128)(2,1)}, bf16[4,32,4096]{2,1,0:T(8,128)(2,1)S(1)}, u32[]{:S(2)}, u32[]{:S(2)}) collective-permute-start(bf16[4,32,4096]{2,1,0:T(8,128)(2,1)} %param.6), channel_id=1, source_target_pairs={{0,1},{1,2},{2,3},{3,4},{4,5},{5,6},{6,7},{7,0},{8,9},{9,10},{10,1... | collective-permute-start | bytes 3145736 | tf_op jit(solution)/shard_map/ppermute | solution.py:24
  36.6 0.9 copy-start.4
  37.6 25.6 %collective-permute-start.1 = (bf16[4,32,4096]{2,1,0:T(8,128)(2,1)S(1)}, bf16[4,32,4096]{2,1,0:T(8,128)(2,1)S(1)}, u32[]{:S(2)}, u32[]{:S(2)}) collective-permute-start(bf16[4,32,4096]{2,1,0:T(8,128)(2,1)S(1)} %collective-permute-done), channel_id=1, source_target_pairs={{0,1},{1,2},{2,3},{3,4},{4,5},{5,6},{6,7},{7,0},{8,9},{9,10},{10,1... | collective-permute-start | bytes 3145736 | tf_op jit(solution)/shard_map/ppermute | solution.py:24
  37.6 26.5 %collective-permute-start.4 = (bf16[4,32,4096]{2,1,0:T(8,128)(2,1)}, bf16[4,32,4096]{2,1,0:T(8,128)(2,1)}, u32[]{:S(2)}, u32[]{:S(2)}) collective-permute-start(bf16[4,32,4096]{2,1,0:T(8,128)(2,1)} %param.6), channel_id=1, source_target_pairs={{1,0},{2,1},{3,2},{4,3},{5,4},{6,5},{7,6},{0,7},{9,8},{10,9},{11,1... | collective-permute-start | bytes 3145736 | tf_op jit(solution)/shard_map/ppermute | solution.py:26
  63.1 1.0 copy-start.6
  64.1 24.7 %collective-permute-start.2 = (bf16[4,32,4096]{2,1,0:T(8,128)(2,1)S(1)}, bf16[4,32,4096]{2,1,0:T(8,128)(2,1)}, u32[]{:S(2)}, u32[]{:S(2)}) collective-permute-start(bf16[4,32,4096]{2,1,0:T(8,128)(2,1)S(1)} %collective-permute-done.1), channel_id=1, source_target_pairs={{0,1},{1,2},{2,3},{3,4},{4,5},{5,6},{6,7},{7,0},{8,9},{9,10},{10,1... | collective-permute-start | bytes 3145736 | tf_op jit(solution)/shard_map/ppermute | solution.py:24
  64.1 33.0 %collective-permute-start.5 = (bf16[4,32,4096]{2,1,0:T(8,128)(2,1)}, bf16[4,32,4096]{2,1,0:T(8,128)(2,1)}, u32[]{:S(2)}, u32[]{:S(2)}) collective-permute-start(bf16[4,32,4096]{2,1,0:T(8,128)(2,1)} %collective-permute-done.4), channel_id=1, source_target_pairs={{1,0},{2,1},{3,2},{4,3},{5,4},{6,5},{7,6},{0,7},{9,8},{10,9},{11,1... | collective-permute-start | bytes 3145736 | tf_op jit(solution)/shard_map/ppermute | solution.py:26
  88.8 24.0 %collective-permute-start.3 = (bf16[4,32,4096]{2,1,0:T(8,128)(2,1)}, bf16[4,32,4096]{2,1,0:T(8,128)(2,1)}, u32[]{:S(2)}, u32[]{:S(2)}) collective-permute-start(bf16[4,32,4096]{2,1,0:T(8,128)(2,1)} %collective-permute-done.2), channel_id=1, source_target_pairs={{0,1},{1,2},{2,3},{3,4},{4,5},{5,6},{6,7},{7,0},{8,9},{9,10},{10,1... | collective-permute-start | bytes 3145736 | tf_op jit(solution)/shard_map/ppermute | solution.py:24
  92.1 27.6 %copy-start.2 = (bf16[4,32,4096]{2,1,0:T(8,128)(2,1)S(1)}, bf16[4,32,4096]{2,1,0:T(8,128)(2,1)}, u32[]{:S(2)}) copy-start(bf16[4,32,4096]{2,1,0:T(8,128)(2,1)} %param.6) | copy-start | bytes 3145732
  95.6 21.9 %copy-start.7 = (bf16[4,32,4096]{2,1,0:T(8,128)(2,1)S(1)}, bf16[4,32,4096]{2,1,0:T(8,128)(2,1)}, u32[]{:S(2)}) copy-start(bf16[4,32,4096]{2,1,0:T(8,128)(2,1)} %copy-done.6) | copy-start | bytes 3145732
  95.6 22.9 %copy-start.5 = (bf16[4,32,4096]{2,1,0:T(8,128)(2,1)S(1)}, bf16[4,32,4096]{2,1,0:T(8,128)(2,1)}, u32[]{:S(2)}) copy-start(bf16[4,32,4096]{2,1,0:T(8,128)(2,1)} %copy-done.4) | copy-start | bytes 3145732
  97.1 28.2 %collective-permute-start.6 = (bf16[4,32,4096]{2,1,0:T(8,128)(2,1)}, bf16[4,32,4096]{2,1,0:T(8,128)(2,1)S(1)}, u32[]{:S(2)}, u32[]{:S(2)}) collective-permute-start(bf16[4,32,4096]{2,1,0:T(8,128)(2,1)} %collective-permute-done.5), channel_id=1, source_target_pairs={{1,0},{2,1},{3,2},{4,3},{5,4},{6,5},{7,6},{0,7},{9,8},{10,9},{11,1... | collective-permute-start | bytes 3145736 | tf_op jit(solution)/shard_map/ppermute | solution.py:26
  134.8 23.8 %copy-start.3 = (bf16[4,32,64,64]{3,2,1,0:T(8,128)(2,1)S(1)}, bf16[4,32,64,64]{3,2,1,0:T(8,128)(2,1)}, u32[]{:S(2)}) copy-start(bf16[4,32,64,64]{3,2,1,0:T(8,128)(2,1)} %broadcast_multiply_fusion) | copy-start | bytes 3145732
  204.2 53.4 %copy-start.1 = (bf16[64,64,64]{2,1,0:T(8,128)(2,1)S(1)}, bf16[64,64,64]{2,1,0:T(8,128)(2,1)}, u32[]{:S(2)}) copy-start(bf16[64,64,64]{2,1,0:T(8,128)(2,1)} %param.8) | copy-start | bytes 1572868
Sparse Core Ops, SparseCore 0:
  10.0 120.0 all-gather.1
  220.5 35.7 reduce-scatter.1
